TPU v7x, 32 devices: a whole 2x2x4 slice. The times are simulated.
32 devices in a mesh: groups: 2 (over y), path: 4 (over z), half: 2 (over x), tile: 2 (over core).
Axes of the slice: x: 2, y: 2, z: 4, core: 2. Of those that a mesh axis runs over, the one named last changes fastest.
Arguments:
- left_prefix: bfloat16 [64, 4096], P(('groups', 'path'), ('half', 'tile')), parts along dimension 0, may hold values from -6 to 6
- right_prefix: bfloat16 [64, 4096], P(('groups', 'half', 'tile'), 'path'), parts along dimension 0, may hold values from -6 to 6
- left_layer: bfloat16 [2048, 1024], P(('groups', 'half', 'tile')), parts along dimension 0, may hold values from -0.1875 to 0.1875
- right_layer: bfloat16 [2048, 1024], P(('groups', 'path')), parts along dimension 0, may hold values from -0.1875 to 0.1875
- left_map: int32 [512], P('groups'), parts along dimension 0, may hold values from 0 to 31
- right_map: int32 [512], P('groups'), parts along dimension 0, may hold values from 0 to 31
- branch_bits: int32 [512, 10], P('groups'), parts along dimension 0, may hold values 0 or 1
- cut_side: int32 [20], P('groups'), parts along dimension 0, may hold values 0 or 1
Outputs:
- amplitude: bfloat16 [8192, 4096], P(('groups', 'half', 'tile'), 'path'), parts along dimension 0
There are 2 independent parts, one for each index of `groups`. A program takes and returns all parts, laid end to end along the dimension named above; each array names one. Nothing has to cross between parts.
All inputs are finite; a program needn't handle non-finite values.
Results may differ from a plain program's by a relative error of at most 0.0058.
Values may be sent and summed in bfloat16 or wider, within the bound.
A program may use at most 64 MiB of HBM per device.

v0:
```python
import jax
import jax.numpy as jnp
from jax import lax
from jax.sharding import PartitionSpec as P


def cut_factors(branch, cut_side, gate_count, on_left):
    cut_count = cut_side.shape[0]
    bit_place = lax.broadcasted_iota(jnp.int32, (cut_count, gate_count), 0)
    gate_code = lax.broadcasted_iota(jnp.int32, (cut_count, gate_count), 1)
    bit_table = jnp.right_shift(gate_code, bit_place) & 1
    projector = cut_side if on_left else 1 - cut_side
    phased = 1 - projector
    chosen = branch * projector[None, :]
    misses = (
        jnp.sum(chosen, axis=1, keepdims=True)
        + jnp.dot(projector, bit_table)[None, :]
        - 2 * jnp.dot(chosen, bit_table)
    )
    parity = jnp.dot(branch * phased[None, :], bit_table)
    sign_value = 1 - 2 * (parity % 2)
    return jnp.where(misses == 0, sign_value, 0).astype(jnp.bfloat16)


def project(prefix_rows, path_map, branch, cut_side, on_left):
    factor = cut_factors(branch, cut_side, prefix_rows.shape[1], on_left)
    return prefix_rows[path_map] * factor


def apply_left(projected, left_layer):

    def columns(layer_piece, first_row):
        return lax.dot_general(
            projected, layer_piece, (((1,), (1,)), ((), ())), preferred_element_type=jnp.float32
        )

    states = columns(lax.all_gather(left_layer, ("half", "tile"), axis=0, tiled=True), jnp.int32(0))
    return states.astype(jnp.bfloat16)


def apply_right(projected, right_layer):

    def columns(layer_piece, first_row):
        return lax.dot_general(
            projected, layer_piece, (((1,), (1,)), ((), ())), preferred_element_type=jnp.float32
        )

    states = columns(lax.all_gather(right_layer, "path", axis=0, tiled=True), jnp.int32(0))
    return states.astype(jnp.bfloat16)


def on_device(
    left_prefix, right_prefix, left_layer, right_layer, left_map, right_map, branch_bits, cut_side
):
    left_rows = lax.all_gather(left_prefix, "path", axis=0, tiled=True)
    right_rows = lax.all_gather(right_prefix, ("half", "tile"), axis=0, tiled=True)
    left_states = apply_left(project(left_rows, left_map, branch_bits, cut_side, True), left_layer)
    right_states = apply_right(
        project(right_rows, right_map, branch_bits, cut_side, False), right_layer
    )
    amplitude = lax.dot_general(
        left_states, right_states, (((0,), (0,)), ((), ())), preferred_element_type=jnp.float32
    )
    return amplitude.astype(jnp.bfloat16)


def solution(mesh):
    in_specs = (
        P(("groups", "path"), ("half", "tile")),
        P(("groups", "half", "tile"), "path"),
        P(("groups", "half", "tile"), None),
        P(("groups", "path"), None),
        P("groups"),
        P("groups"),
        P("groups", None),
        P("groups"),
    )
    out_specs = P(("groups", "half", "tile"), "path")
    return jax.shard_map(
        on_device, mesh=mesh, in_specs=in_specs, out_specs=out_specs, check_vma=False
    )
```

profile of v0, /device:TPU:1, one launch (start us, length us, event | category | flops | bytes accessed | tf_op | source)
XLA Modules:
  0.0 92.6 jit_solution(1956754094180607474)
XLA Ops:
  6.5 0.0 all-gather.5.cloned.1.call-start
  6.5 0.7 all-gather.5.cloned.1.call-update
  7.3 0.0 all-gather.3.cloned.1.call-start
  7.3 0.7 all-gather.3.cloned.1.call-update
  8.0 6.3 %all_gather.14 = bf16[32,1024]{1,0:T(8,128)(2,1)S(1)} all-gather(bf16[8,1024]{1,0:T(8,128)(2,1)} %param.9), channel_id=1, replica_groups=mesh['groups'=2,'path'=4,'half'=2,'tile'=2] {'half','tile'}, dimensions={0}, use_global_device_ids=true | all-gather | bytes 81920 | tf_op jit(solution)/shard_map/all_gather | solution.py:56
  14.3 0.7 compare_select_fusion
  15.0 0.0 copy-start.1
  15.0 0.0 copy-start.3
  15.0 1.2 %gather_fusion.1 = bf16[256,1024]{1,0:T(8,128)(2,1)S(1)} fusion(bf16[32,1024]{1,0:T(8,128)(2,1)S(1)} %all_gather.14, s32[1024]{0:T(1024)S(1)} %pad_clamp_fusion), kind=kCustom, calls=%fused_computation.1 | custom fusion | bytes 1049600 | tf_op jit(solution)/shard_map/gather | solution.py:27
  16.2 0.0 copy-done.1
  16.2 12.1 %all_gather.12 = bf16[32,1024]{1,0:T(8,128)(2,1)S(1)} all-gather(bf16[8,1024]{1,0:T(8,128)(2,1)S(1)} %copy-done.1), channel_id=1, replica_groups=mesh['groups'=2,'path'=4,'half'=2,'tile'=2] {'path'}, dimensions={0}, use_global_device_ids=true | all-gather | bytes 81920 | tf_op jit(solution)/shard_map/all_gather | solution.py:55
  28.3 0.0 copy-done.3
  28.4 0.0 copy-start.2
  28.4 0.0 copy-start
  28.4 1.2 %gather_fusion = bf16[256,1024]{1,0:T(8,128)(2,1)S(1)} fusion(bf16[32,1024]{1,0:T(8,128)(2,1)S(1)} %all_gather.12, s32[1024]{0:T(1024)S(1)} %pad_clamp_fusion.1), kind=kCustom, calls=%fused_computation | custom fusion | bytes 1049600 | tf_op jit(solution)/shard_map/gather | solution.py:27
  29.6 0.0 copy-done.2
  29.6 0.0 copy-done
  29.6 0.1 multiply_reduce_fusion.1
  29.7 0.2 fusion.28
  29.9 0.2 fusion.31
  30.1 1.7 %fusion.29 = s32[256,1024]{1,0:T(8,128)S(1)} fusion(s32[256,10]{0,1:T(8,128)S(1)} %copy-done, s32[10]{0:T(128)S(1)} %broadcast_subtract_fusion), kind=kOutput, calls=%fused_computation.35 | convolution fusion | flops 5265920 | bytes 1058856 | tf_op jit(solution)/shard_map/dot_general | solution.py:20
  31.7 1.7 %fusion.30 = s32[256,1024]{1,0:T(8,128)S(1)} fusion(s32[256,10]{0,1:T(8,128)S(1)} %copy-done, s32[10]{0:T(128)S(1)} %copy-done.2), kind=kOutput, calls=%fused_computation.36 | convolution fusion | flops 5265920 | bytes 1058856 | tf_op jit(solution)/shard_map/dot_general | solution.py:18
  33.4 23.8 %all-gather.5.cloned.1.call-done = bf16[1024,1024]{1,0:T(8,128)(2,1)} async-done(((bf16[256,1024]{1,0:T(8,128)(2,1)}), bf16[1024,1024]{1,0:T(8,128)(2,1)}) %all-gather.5.cloned.1.call-update) | async-done | bytes 2097168 | tf_op jit(solution)/shard_map/all_gather | solution.py:48
  57.2 3.6 %convolution_convert_fusion.1 = bf16[256,1024]{1,0:T(8,128)(2,1)} fusion(bf16[1024,1024]{1,0:T(8,128)(2,1)} %all-gather.5.cloned.1.call-done, bf16[256,1024]{1,0:T(8,128)(2,1)S(1)} %gather_fusion.1, s32[256,1024]{1,0:T(8,128)S(1)} %fusion.29, s32[256,1024]{1,0:T(8,128)S(1)} %fusion.30, s32[1024]{0:T(1024)S(1)} %bitcast.12, s32[256]{0:T(256)S(1)} %get-tuple-element.6), kind=kOutput, calls=%fused_computation.9 | convolution fusion | flops 543162368 | bytes 5248000 | tf_op jit(solution)/shard_map/dot_general | solution.py:44
  60.9 20.0 %all-gather.3.cloned.1.call-done = bf16[1024,1024]{1,0:T(8,128)(2,1)} async-done(((bf16[256,1024]{1,0:T(8,128)(2,1)}), bf16[1024,1024]{1,0:T(8,128)(2,1)}) %all-gather.3.cloned.1.call-update) | async-done | bytes 2097168 | tf_op jit(solution)/shard_map/all_gather | solution.py:37
  80.9 4.8 %convolution_convert_fusion = bf16[1024,1024]{1,0:T(8,128)(2,1)} fusion(bf16[256,1024]{1,0:T(8,128)(2,1)} %convolution_convert_fusion.1, bf16[1024,1024]{1,0:T(8,128)(2,1)} %all-gather.3.cloned.1.call-done, bf16[256,1024]{1,0:T(8,128)(2,1)S(1)} %gather_fusion, s32[256,1024]{1,0:T(8,128)S(1)} %fusion.30, s32[256,1024]{1,0:T(8,128)S(1)} %fusion.29, ...), kind=kOutput, calls=%fused_computation.2 | convolution fusion | flops 1081081856 | bytes 7345152 | tf_op jit(solution)/shard_map/dot_general | solution.py:61
  (4 shorter events, 0.0 us)
Async XLA Ops:
  6.5 50.7 %all-gather.5.cloned.1.call-start = ((), (), s32[]{:S(2)}) async-start(), calls=%async_computation.1 | async-start | bytes 2621440 | tf_op jit(solution)/shard_map/all_gather | solution.py:48
  7.3 73.6 %all-gather.3.cloned.1.call-start = ((), (), s32[]{:S(2)}) async-start(), calls=%async_computation | async-start | bytes 2621440 | tf_op jit(solution)/shard_map/all_gather | solution.py:37
  15.0 1.2 %copy-start.1 = (bf16[8,1024]{1,0:T(8,128)(2,1)S(1)}, bf16[8,1024]{1,0:T(8,128)(2,1)}, u32[]{:S(2)}) copy-start(bf16[8,1024]{1,0:T(8,128)(2,1)} %param.8) | copy-start | bytes 49156
  15.0 13.3 %copy-start.3 = (s32[256]{0:T(256)S(1)}, s32[256]{0:T(256)}, u32[]{:S(2)}) copy-start(s32[256]{0:T(256)} %param.12) | copy-start | bytes 3076
  28.4 1.2 %copy-start.2 = (s32[10]{0:T(128)S(1)}, s32[10]{0:T(128)}, u32[]{:S(2)}) copy-start(s32[10]{0:T(128)} %param.15) | copy-start | bytes 124
  28.4 1.2 %copy-start = (s32[256,10]{0,1:T(8,128)S(1)}, s32[256,10]{0,1:T(8,128)}, u32[]{:S(2)}) copy-start(s32[256,10]{0,1:T(8,128)} %param.14) | copy-start | bytes 30724
Sparse Core Ops, SparseCore 0:
  8.9 48.2 all-gather.4
  58.8 22.0 all-gather.2
where the time goes:
time: 93 us; the launch traced here: 92.6 us
  waiting for transfers between devices  45.3 us (49%)
  blocking collectives  18.4 us (20%)
  between operations  13.5 us (15%)
  matrix products  12.2 us (13%)
  local copies, waits for them, and re-layouts  2.36 us (3%)
    all_gather x1, waiting for transfers between devices, apply_right(): lax.all_gather(right_layer, 'path', axis=0, tiled=True)  23.8 us
    all_gather x1, waiting for transfers between devices, apply_left(): lax.all_gather(left_layer, ('half', 'tile'), axis=0, tiled=True)  20 us
    all_gather x1, blocking collectives, on_device(): left_rows = lax.all_gather(left_prefix, 'path', axis=0, tiled=True)  12.1 us
    all_gather x1, blocking collectives, on_device(): lax.all_gather(right_prefix, ('half', 'tile'), axis=0, tiled=True)  6.31 us
    dot_general x1, matrix products, on_device(): lax.dot_general(left_states, right_states, (((0,), (0,)), ((), ())), pref...  4.83 us
    dot_general x1, matrix products, columns(): lax.dot_general(projected, layer_piece, (((1,), (1,)), ((), ())), preferr...  3.64 us
    gather x2, local copies, waits for them, and re-layouts, project(): return prefix_rows[path_map] * factor  2.34 us
  transfers between devices with their start and end apart: 2, of which 2 were waited for; matrix products, arithmetic and copies ran while one was open for 11% of the time, Pallas kernels for 0%

commit v1 on v0

v1 whole, which is shorter than its diff:
```python
import functools

import jax
import jax.numpy as jnp
from jax import lax
from jax.experimental import pallas as pl
from jax.experimental.pallas import tpu as pltpu
from jax.sharding import PartitionSpec as P

MESH = pl.DeviceIdType.MESH
NT = (((1,), (1,)), ((), ()))


def factors(branch, side, gate_count):
    cuts = branch.shape[1]
    place = lax.broadcasted_iota(jnp.int32, (cuts, gate_count), 0)
    code = lax.broadcasted_iota(jnp.int32, (cuts, gate_count), 1)
    bits = (jnp.right_shift(code, place) & 1).astype(jnp.float32).astype(jnp.bfloat16)

    def dot(rows):
        return jnp.dot(rows.astype(jnp.bfloat16), bits, preferred_element_type=jnp.float32)

    made = []
    for projector in (side, 1.0 - side):
        chosen = branch * projector
        misses = jnp.sum(chosen, axis=1, keepdims=True) + dot(projector - 2.0 * chosen)
        parity = dot(branch - chosen).astype(jnp.int32) & 1
        sign = (1 - 2 * parity).astype(jnp.float32)
        made.append(jnp.where(misses == 0.0, sign, 0.0))
    return made


def picked_rows(prefix_ref, path_map):
    shards, rows, gate_count = prefix_ref.shape
    prefix = prefix_ref[...].astype(jnp.float32).reshape(shards * rows, gate_count)
    which = lax.broadcasted_iota(jnp.int32, (shards * rows, path_map.shape[1]), 0)
    hot = jnp.where(which == path_map, 1.0, 0.0).T
    return jnp.dot(
        hot.astype(jnp.bfloat16), prefix.astype(jnp.bfloat16), preferred_element_type=jnp.float32
    )


def kernel(
    sizes,
    left_prefix, right_prefix, left_layer, right_layer, left_map, right_map, branch_bits, cut_side,
    left_out, right_out,
    left_rows, right_rows, left_proj, right_proj, left_w, right_w,
    own_sem, pre_send, pre_recv,
    r_send, r_recv, r_sib_send, r_sib_recv,
    l_send, l_recv, l_sib_send, l_sib_recv, o_send, o_recv,
):
    n_half, n_path, n_tile = sizes
    x, z, c = lax.axis_index("half"), lax.axis_index("path"), lax.axis_index("tile")
    sib = 1 - c
    n_lr = n_half * n_tile
    mine = x * n_tile + c

    barrier = pltpu.get_barrier_semaphore()
    for k in range(1, n_path):
        pl.semaphore_signal(
            barrier, inc=1, device_id={"path": lax.rem(z + k, n_path)}, device_id_type=MESH
        )
    for k in range(1, n_lr):
        there = lax.rem(mine + k, n_lr)
        pl.semaphore_signal(
            barrier,
            inc=1,
            device_id={"half": there // n_tile, "tile": lax.rem(there, n_tile)},
            device_id_type=MESH,
        )

    block_l, gate = left_layer.shape
    block_r = right_layer.shape[0]
    part_r = block_r // n_tile
    chunk_r = max(16, part_r // 2)
    chunk_l = max(16, block_l // 4)
    count_r, count_l = part_r // chunk_r, block_l // chunk_l

    own = [
        pltpu.make_async_copy(left_prefix, left_rows.at[z], own_sem.at[0]),
        pltpu.make_async_copy(right_prefix, right_rows.at[mine], own_sem.at[1]),
        pltpu.make_async_copy(
            left_layer, left_w.at[pl.ds(pl.multiple_of(mine * block_l, block_l), block_l)], own_sem.at[2]
        ),
        pltpu.make_async_copy(
            right_layer, right_w.at[pl.ds(pl.multiple_of(z * block_r, block_r), block_r)], own_sem.at[3]
        ),
    ]
    for copy in own:
        copy.start()

    side = cut_side[...].astype(jnp.float32)
    branch = branch_bits[...].astype(jnp.float32)
    for ref, factor in zip((left_proj, right_proj), factors(branch, side, gate)):
        ref[...] = factor.astype(jnp.bfloat16)

    pl.semaphore_wait(barrier, n_path - 1 + n_lr - 1)

    def remote(src, dst, send, recv, device):
        return pltpu.make_async_remote_copy(
            src_ref=src, dst_ref=dst, send_sem=send, recv_sem=recv, device_id=device, device_id_type=MESH
        )

    prefix_copies = []
    for k in range(1, n_path):
        prefix_copies.append(remote(
            left_prefix, left_rows.at[z], pre_send.at[k - 1], pre_recv.at[k - 1],
            {"path": lax.rem(z + k, n_path)},
        ))
    for k in range(1, n_lr):
        there = lax.rem(mine + k, n_lr)
        slot = n_path - 1 + k - 1
        prefix_copies.append(remote(
            right_prefix, right_rows.at[mine], pre_send.at[slot], pre_recv.at[slot],
            {"half": there // n_tile, "tile": lax.rem(there, n_tile)},
        ))
    for copy in prefix_copies:
        copy.start()

    def rows_r(block, core, i):
        return pl.ds(pl.multiple_of(block * block_r + core * part_r + i * chunk_r, chunk_r), chunk_r)

    def rows_l(block, core, i):
        return pl.ds(
            pl.multiple_of((block * n_tile + core) * block_l + i * chunk_l, chunk_l), chunk_l
        )

    class Line:
        def __init__(self, axis, pos, n, rows, buf, first, out, proj, count, sems):
            self.axis, self.pos, self.n, self.rows, self.buf = axis, pos, n, rows, buf
            self.first, self.out, self.proj, self.count = first, out, proj, count
            self.send, self.recv, self.sib_send, self.sib_recv = sems
            self.slots = (n - 1) * count

        def block(self, way, d):
            return self.pos - d if way == 0 else self.pos + d

        def has(self, way, d):
            return (self.pos >= d) if way == 0 else (self.pos + d < self.n)

        def sends(self, way, d):
            onward = (self.pos + 1 < self.n) if way == 0 else (self.pos >= 1)
            return jnp.logical_and(self.has(way, d), onward)

        def onward(self, way, d, i, own=False):
            span = self.rows(self.block(way, d), c, i)
            src = self.first(i) if own else self.buf.at[span]
            at = d * self.count + i
            return remote(
                src, self.buf.at[span], self.send.at[way, at], self.recv.at[way, at],
                {self.axis: self.pos + (1 if way == 0 else -1)},
            )

        def arrived(self, way, d, i):
            span = self.rows(self.block(way, d), c, i)
            at = (d - 1) * self.count + i
            return remote(
                self.buf.at[span], self.buf.at[span], self.send.at[way, at], self.recv.at[way, at],
                {self.axis: self.pos + (1 if way == 0 else -1)},
            )

        def share(self, way, d, i, core):
            span = self.rows(self.block(way, d), core, i)
            at = (d - 1) * self.count + i
            return remote(
                self.buf.at[span], self.buf.at[span],
                self.sib_send.at[way, at], self.sib_recv.at[way, at], {"tile": sib},
            )

        def start_own(self, i):
            for way in (0, 1):
                @pl.when(self.sends(way, 0))
                def _():
                    self.onward(way, 0, i, own=True).start()

        def relay(self, s):
            d, i = s // self.count + 1, lax.rem(s, self.count)
            for way in (0, 1):
                @pl.when(jnp.logical_and(s < self.slots, self.has(way, d)))
                def _():
                    self.arrived(way, d, i).wait_recv()
                    @pl.when(jnp.logical_and(self.sends(way, d), d < self.n - 1))
                    def _():
                        self.onward(way, d, i).start()
                    self.share(way, d, i, c).start()

        def multiply(self, span):
            self.out[span, :] = lax.dot_general(
                self.buf[span, :], self.proj[...], NT, preferred_element_type=jnp.float32
            ).astype(self.out.dtype)

        def compute(self, s):
            d, i = s // self.count + 1, lax.rem(s, self.count)
            for way in (0, 1):
                @pl.when(jnp.logical_and(s < self.slots, self.has(way, d)))
                def _():
                    self.multiply(self.rows(self.block(way, d), c, i))

        def compute_shared(self, s):
            d, i = s // self.count + 1, lax.rem(s, self.count)
            for way in (0, 1):
                @pl.when(jnp.logical_and(jnp.logical_and(s >= 0, s < self.slots), self.has(way, d)))
                def _():
                    self.share(way, d, i, sib).wait_recv()
                    self.multiply(self.rows(self.block(way, d), sib, i))

        def finish(self, s):
            d, i = s // self.count, lax.rem(s, self.count)
            for way in (0, 1):
                @pl.when(self.sends(way, d))
                def _():
                    self.onward(way, d, i).wait_send()
                @pl.when(self.has(way, d + 1))
                def _():
                    self.share(way, d + 1, i, c).wait_send()

    right = Line(
        "path", z, n_path, rows_r, right_w,
        lambda i: right_layer.at[pl.ds(pl.multiple_of(c * part_r + i * chunk_r, chunk_r), chunk_r)],
        right_out, right_proj, count_r, (r_send, r_recv, r_sib_send, r_sib_recv),
    )
    left = Line(
        "half", x, n_half, rows_l, left_w,
        lambda i: left_layer.at[pl.ds(i * chunk_l, chunk_l)],
        left_out, left_proj, count_l, (l_send, l_recv, l_sib_send, l_sib_recv),
    )

    def own_share(i, core):
        span = rows_l(x, core, i)
        return remote(
            left.first(i), left_w.at[span], o_send.at[i], o_recv.at[i], {"tile": sib}
        )

    for i in range(max(count_r, count_l)):
        if i < count_r:
            right.start_own(i)
        if i < count_l:
            left.start_own(i)
    for i in range(count_l):
        own_share(i, c).start()

    for copy in own:
        copy.wait()
    for copy in prefix_copies:
        copy.wait_recv()
    for ref, rows, path_map in ((left_proj, left_rows, left_map), (right_proj, right_rows, right_map)):
        chosen = picked_rows(rows, path_map[...])
        ref[...] = (chosen * ref[...].astype(jnp.float32)).astype(jnp.bfloat16)

    left.multiply(pl.ds(pl.multiple_of(mine * block_l, block_l), block_l))
    right.multiply(pl.ds(pl.multiple_of(z * block_r, block_r), block_r))

    slots = max(right.slots, left.slots)

    def step(s, _):
        right.relay(s)
        left.relay(s)
        right.compute_shared(s - 1)
        left.compute_shared(s - 1)
        right.compute(s)
        left.compute(s)
        return 0

    def shared_block():
        for i in range(count_l):
            own_share(i, sib).wait_recv()
        left.multiply(pl.ds(pl.multiple_of((x * n_tile + sib) * block_l, block_l), block_l))

    if slots > 0:
        lax.fori_loop(0, 1, step, 0)
    shared_block()
    if slots > 1:
        lax.fori_loop(1, slots, step, 0)
    right.compute_shared(jnp.int32(slots - 1))
    left.compute_shared(jnp.int32(slots - 1))

    for line in (right, left):
        if line.slots > 0:
            lax.fori_loop(0, line.slots, lambda s, _, line=line: (line.finish(s), 0)[1], 0)
    for i in range(count_l):
        own_share(i, c).wait_send()
    for copy in prefix_copies:
        copy.wait_send()


def on_device(
    sizes,
    left_prefix, right_prefix, left_layer, right_layer, left_map, right_map, branch_bits, cut_side,
):
    n_half, n_path, n_tile = sizes
    n_lr = n_half * n_tile
    paths = left_map.shape[0]
    gate = left_layer.shape[1]
    hi_l, hi_r = left_layer.shape[0] * n_lr, right_layer.shape[0] * n_path
    part_r = right_layer.shape[0] // n_tile
    count_r = part_r // max(16, part_r // 2)
    count_l = left_layer.shape[0] // max(16, left_layer.shape[0] // 4)
    slots_r = max(1, (n_path - 1) * count_r)
    slots_l = max(1, (n_half - 1) * count_l)
    pre = n_path + n_lr - 2
    dma = pltpu.SemaphoreType.DMA
    vmem = pl.BlockSpec(memory_space=pltpu.VMEM)
    anywhere = pl.BlockSpec(memory_space=pl.ANY)
    left_states, right_states = pl.pallas_call(
        functools.partial(kernel, sizes),
        out_shape=(
            jax.ShapeDtypeStruct((hi_l, paths), jnp.bfloat16),
            jax.ShapeDtypeStruct((hi_r, paths), jnp.bfloat16),
        ),
        in_specs=[anywhere] * 4 + [vmem] * 4,
        out_specs=(vmem, vmem),
        scratch_shapes=[
            pltpu.VMEM((n_path,) + left_prefix.shape, jnp.bfloat16),
            pltpu.VMEM((n_lr,) + right_prefix.shape, jnp.bfloat16),
            pltpu.VMEM((paths, gate), jnp.bfloat16),
            pltpu.VMEM((paths, gate), jnp.bfloat16),
            pltpu.VMEM((hi_l, gate), jnp.bfloat16),
            pltpu.VMEM((hi_r, gate), jnp.bfloat16),
            dma((4,)), dma((pre,)), dma((pre,)),
            dma((2, slots_r)), dma((2, slots_r)), dma((2, slots_r)), dma((2, slots_r)),
            dma((2, slots_l)), dma((2, slots_l)), dma((2, slots_l)), dma((2, slots_l)),
            dma((count_l,)), dma((count_l,)),
        ],
        compiler_params=pltpu.CompilerParams(collective_id=0, has_side_effects=True),
    )(
        left_prefix, right_prefix, left_layer, right_layer,
        left_map[None, :], right_map[None, :], branch_bits, cut_side[None, :],
    )
    amplitude = lax.dot_general(
        left_states, right_states, NT, preferred_element_type=jnp.float32
    )
    return amplitude.astype(jnp.bfloat16)


def solution(mesh):
    in_specs = (
        P(("groups", "path"), ("half", "tile")),
        P(("groups", "half", "tile"), "path"),
        P(("groups", "half", "tile"), None),
        P(("groups", "path"), None),
        P("groups"),
        P("groups"),
        P("groups", None),
        P("groups"),
    )
    out_specs = P(("groups", "half", "tile"), "path")
    sizes = tuple(mesh.shape[axis] for axis in ("half", "path", "tile"))
    return jax.shard_map(
        functools.partial(on_device, sizes),
        mesh=mesh, in_specs=in_specs, out_specs=out_specs, check_vma=False,
    )
```

time: 93 us -> 33.4 us (0.36)
  waiting for transfers between devices: 45.3 us -> 0 us
  Pallas kernels: 0 us -> 28.4 us
  blocking collectives: 18.4 us -> 0 us
  between operations: 13.5 us -> 0.01 us
  matrix products: 12.2 us -> 3.26 us
    all_gather x2 -> x0, waiting for transfers between devices: 43.9 us -> none  [the longest x1 23.8 us: apply_right(): lax.all_gather(right_layer, 'path', axis=0, tiled=True)]
    pallas_call x0 -> x1, Pallas kernels: none -> 28.4 us  [on_device(): pl.pallas_call(functools.partial(kernel, sizes), out_shape=(jax.ShapeDtyp...]
    all_gather x2 -> x0, blocking collectives: 18.4 us -> none  [the longest x1 12.1 us: on_device(): left_rows = lax.all_gather(left_prefix, 'path', axis=0, tiled=True)]
    dot_general x6 -> x1, matrix products: 12.2 us -> 3.26 us  [on_device(): lax.dot_general(left_states, right_states, NT, preferred_element_type=jnp...]
    gather x2 -> x0, local copies, waits for them, and re-layouts: 2.34 us -> none  [project(): return prefix_rows[path_map] * factor]
    unnamed x8 -> x1, local copies, waits for them, and re-layouts: 0.02 us -> 1.48 us
    unnamed x2 -> x0, waiting for transfers between devices: 1.41 us -> none
  transfers between devices with their start and end apart: 2 -> 0, of which waited for: 2 -> 0; matrix products, arithmetic and copies ran while one was open for 11% -> 0% of each run, Pallas kernels for 0% -> 0%
where the time goes in v1:
time: 33.4 us; the launch traced here: 33.2 us
  Pallas kernels  28.4 us (85%)
  matrix products  3.26 us (10%)
  local copies, waits for them, and re-layouts  1.48 us (4%)
    pallas_call x1, Pallas kernels, on_device(): pl.pallas_call(functools.partial(kernel, sizes), out_shape=(jax.ShapeDtyp...  28.4 us
    dot_general x1, matrix products, on_device(): lax.dot_general(left_states, right_states, NT, preferred_element_type=jnp...  3.26 us
    unnamed x1, local copies, waits for them, and re-layouts  1.48 us

profile of v1, /device:TPU:1, one launch (start us, length us, event | category | flops | bytes accessed | tf_op | source)
XLA Modules:
  0.0 33.2 jit_solution(17041067140801523118)
XLA Ops:
  0.0 1.5 %copy.9.branch_bits = s32[256,10]{1,0:T(8,128)} copy(s32[256,10]{0,1:T(8,128)} %param.14) | data formatting | bytes 20480 | tf_op args[6]
  1.5 28.4 %shard_map.82 = (bf16[1024,256]{1,0:T(8,128)(2,1)}, bf16[1024,256]{1,0:T(8,128)(2,1)}) custom-call(bf16[8,1024]{1,0:T(8,128)(2,1)} %left_prefix.1, bf16[8,1024]{1,0:T(8,128)(2,1)} %right_prefix.1, bf16[256,1024]{1,0:T(8,128)(2,1)} %left_layer.1, bf16[256,1024]{1,0:T(8,128)(2,1)} %right_layer.1, s32[1,256]{1,0:T(1,128)} %bitcast.5, s32[1,256]{1,0:T(1,128)} %bitcast.6, ...), custom_call_target="tpu_custom_call" | custom-call | tf_op jit(solution)/shard_map/pallas_call | solution.py:304
  29.9 3.3 %convolution_convert_fusion = bf16[1024,1024]{1,0:T(8,128)(2,1)} fusion(bf16[1024,256]{1,0:T(8,128)(2,1)} %get-tuple-element.7, bf16[1024,256]{1,0:T(8,128)(2,1)} %get-tuple-element.8), kind=kOutput, calls=%fused_computation | convolution fusion | flops 537919488 | bytes 3145728 | tf_op jit(solution)/shard_map/dot_general | solution.py:329

commit v2 on v1

--- a/solution.py
+++ b/solution.py
@@ -9,30 +9,37 @@
 
 MESH = pl.DeviceIdType.MESH
 NT = (((1,), (1,)), ((), ()))
-
-
-def factors(branch, side, gate_count):
-    cuts = branch.shape[1]
+TN = (((0,), (0,)), ((), ()))
+
+
+def factors(branch, side_row, gate_count):
+    cuts = branch.shape[0]
+    across = lax.broadcasted_iota(jnp.int32, (cuts, cuts), 0)
+    down = lax.broadcasted_iota(jnp.int32, (cuts, cuts), 1)
+    side = jnp.sum(jnp.where(across == down, side_row, 0.0), axis=1, keepdims=True)
     place = lax.broadcasted_iota(jnp.int32, (cuts, gate_count), 0)
     code = lax.broadcasted_iota(jnp.int32, (cuts, gate_count), 1)
-    bits = (jnp.right_shift(code, place) & 1).astype(jnp.float32).astype(jnp.bfloat16)
-
-    def dot(rows):
-        return jnp.dot(rows.astype(jnp.bfloat16), bits, preferred_element_type=jnp.float32)
+    bits = (jnp.right_shift(code, place) & 1).astype(jnp.float32)
+
+    def dot(columns, table):
+        return lax.dot_general(
+            columns.astype(jnp.bfloat16), table.astype(jnp.bfloat16), TN,
+            preferred_element_type=jnp.float32,
+        )
 
     made = []
     for projector in (side, 1.0 - side):
         chosen = branch * projector
-        misses = jnp.sum(chosen, axis=1, keepdims=True) + dot(projector - 2.0 * chosen)
-        parity = dot(branch - chosen).astype(jnp.int32) & 1
+        misses = dot(chosen, 1.0 - bits) + dot(projector - chosen, bits)
+        parity = dot(branch - chosen, bits).astype(jnp.int32) & 1
         sign = (1 - 2 * parity).astype(jnp.float32)
         made.append(jnp.where(misses == 0.0, sign, 0.0))
     return made
 
 
-def picked_rows(prefix_ref, path_map):
-    shards, rows, gate_count = prefix_ref.shape
-    prefix = prefix_ref[...].astype(jnp.float32).reshape(shards * rows, gate_count)
+def picked_rows(prefix, path_map):
+    shards, rows, gate_count = prefix.shape
+    prefix = prefix.astype(jnp.float32).reshape(shards * rows, gate_count)
     which = lax.broadcasted_iota(jnp.int32, (shards * rows, path_map.shape[1]), 0)
     hot = jnp.where(which == path_map, 1.0, 0.0).T
     return jnp.dot(
@@ -44,10 +51,12 @@
     sizes,
     left_prefix, right_prefix, left_layer, right_layer, left_map, right_map, branch_bits, cut_side,
     left_out, right_out,
-    left_rows, right_rows, left_proj, right_proj, left_w, right_w,
+    left_rows, right_rows, left_proj, right_factor, right_proj, left_w, right_w,
+    left_st, right_st, stage,
     own_sem, pre_send, pre_recv,
-    r_send, r_recv, r_sib_send, r_sib_recv,
-    l_send, l_recv, l_sib_send, l_sib_recv, o_send, o_recv,
+    pz_send, pz_recv, ps_send, ps_recv,
+    st_send, st_recv, ss_send, ss_recv,
+    l_send, l_recv, l_sib_send, l_sib_recv, o_send, o_recv, lo_sem, ro_sem,
 ):
     n_half, n_path, n_tile = sizes
     x, z, c = lax.axis_index("half"), lax.axis_index("path"), lax.axis_index("tile")
@@ -72,26 +81,24 @@
     block_l, gate = left_layer.shape
     block_r = right_layer.shape[0]
     part_r = block_r // n_tile
-    chunk_r = max(16, part_r // 2)
     chunk_l = max(16, block_l // 4)
-    count_r, count_l = part_r // chunk_r, block_l // chunk_l
+    count_l = block_l // chunk_l
+    half_lr = n_lr // n_tile
 
     own = [
         pltpu.make_async_copy(left_prefix, left_rows.at[z], own_sem.at[0]),
-        pltpu.make_async_copy(right_prefix, right_rows.at[mine], own_sem.at[1]),
+        pltpu.make_async_copy(right_prefix, right_rows.at[z, mine], own_sem.at[1]),
         pltpu.make_async_copy(
             left_layer, left_w.at[pl.ds(pl.multiple_of(mine * block_l, block_l), block_l)], own_sem.at[2]
         ),
-        pltpu.make_async_copy(
-            right_layer, right_w.at[pl.ds(pl.multiple_of(z * block_r, block_r), block_r)], own_sem.at[3]
-        ),
+        pltpu.make_async_copy(right_layer, right_w, own_sem.at[3]),
     ]
     for copy in own:
         copy.start()
 
     side = cut_side[...].astype(jnp.float32)
     branch = branch_bits[...].astype(jnp.float32)
-    for ref, factor in zip((left_proj, right_proj), factors(branch, side, gate)):
+    for ref, factor in zip((left_proj, right_factor), factors(branch, side, gate)):
         ref[...] = factor.astype(jnp.bfloat16)
 
     pl.semaphore_wait(barrier, n_path - 1 + n_lr - 1)
@@ -111,24 +118,35 @@
         there = lax.rem(mine + k, n_lr)
         slot = n_path - 1 + k - 1
         prefix_copies.append(remote(
-            right_prefix, right_rows.at[mine], pre_send.at[slot], pre_recv.at[slot],
+            right_prefix, right_rows.at[z, mine], pre_send.at[slot], pre_recv.at[slot],
             {"half": there // n_tile, "tile": lax.rem(there, n_tile)},
         ))
     for copy in prefix_copies:
         copy.start()
 
-    def rows_r(block, core, i):
-        return pl.ds(pl.multiple_of(block * block_r + core * part_r + i * chunk_r, chunk_r), chunk_r)
-
     def rows_l(block, core, i):
         return pl.ds(
             pl.multiple_of((block * n_tile + core) * block_l + i * chunk_l, chunk_l), chunk_l
         )
 
+    def left_flush(block, core, i):
+        span = rows_l(block, core, i)
+        at = (block * n_tile + core) * count_l + i
+        return pltpu.make_async_copy(left_st.at[span], left_out.at[span], lo_sem.at[at])
+
+    def part(block, core):
+        return pl.ds(pl.multiple_of(block * block_r + core * part_r, part_r), part_r)
+
+    def right_flush(block, core):
+        span = part(block, core)
+        return pltpu.make_async_copy(
+            right_st.at[span], right_out.at[span], ro_sem.at[block * n_tile + core]
+        )
+
     class Line:
-        def __init__(self, axis, pos, n, rows, buf, first, out, proj, count, sems):
+        def __init__(self, axis, pos, n, rows, buf, first, proj, count, sems):
             self.axis, self.pos, self.n, self.rows, self.buf = axis, pos, n, rows, buf
-            self.first, self.out, self.proj, self.count = first, out, proj, count
+            self.first, self.proj, self.count = first, proj, count
             self.send, self.recv, self.sib_send, self.sib_recv = sems
             self.slots = (n - 1) * count
 
@@ -184,17 +202,19 @@
                         self.onward(way, d, i).start()
                     self.share(way, d, i, c).start()
 
-        def multiply(self, span):
-            self.out[span, :] = lax.dot_general(
+        def multiply(self, block, core, i):
+            span = self.rows(block, core, i)
+            left_st[span, :] = lax.dot_general(
                 self.buf[span, :], self.proj[...], NT, preferred_element_type=jnp.float32
-            ).astype(self.out.dtype)
+            ).astype(jnp.bfloat16)
+            left_flush(block, core, i).start()
 
         def compute(self, s):
             d, i = s // self.count + 1, lax.rem(s, self.count)
             for way in (0, 1):
                 @pl.when(jnp.logical_and(s < self.slots, self.has(way, d)))
                 def _():
-                    self.multiply(self.rows(self.block(way, d), c, i))
+                    self.multiply(self.block(way, d), c, i)
 
         def compute_shared(self, s):
             d, i = s // self.count + 1, lax.rem(s, self.count)
@@ -202,7 +222,7 @@
                 @pl.when(jnp.logical_and(jnp.logical_and(s >= 0, s < self.slots), self.has(way, d)))
                 def _():
                     self.share(way, d, i, sib).wait_recv()
-                    self.multiply(self.rows(self.block(way, d), sib, i))
+                    self.multiply(self.block(way, d), sib, i)
 
         def finish(self, s):
             d, i = s // self.count, lax.rem(s, self.count)
@@ -214,15 +234,10 @@
                 def _():
                     self.share(way, d + 1, i, c).wait_send()
 
-    right = Line(
-        "path", z, n_path, rows_r, right_w,
-        lambda i: right_layer.at[pl.ds(pl.multiple_of(c * part_r + i * chunk_r, chunk_r), chunk_r)],
-        right_out, right_proj, count_r, (r_send, r_recv, r_sib_send, r_sib_recv),
-    )
     left = Line(
         "half", x, n_half, rows_l, left_w,
         lambda i: left_layer.at[pl.ds(i * chunk_l, chunk_l)],
-        left_out, left_proj, count_l, (l_send, l_recv, l_sib_send, l_sib_recv),
+        left_proj, count_l, (l_send, l_recv, l_sib_send, l_sib_recv),
     )
 
     def own_share(i, core):
@@ -231,56 +246,176 @@
             left.first(i), left_w.at[span], o_send.at[i], o_recv.at[i], {"tile": sib}
         )
 
-    for i in range(max(count_r, count_l)):
-        if i < count_r:
-            right.start_own(i)
-        if i < count_l:
-            left.start_own(i)
+    for i in range(count_l):
+        left.start_own(i)
     for i in range(count_l):
         own_share(i, c).start()
 
-    for copy in own:
-        copy.wait()
-    for copy in prefix_copies:
+    def prefix_half(block, core):
+        return right_rows.at[block, pl.ds(core * half_lr, half_lr)]
+
+    def prefix_out(to):
+        held = prefix_half(z, c)
+        return remote(held, held, pz_send.at[to], pz_recv.at[z], {"path": to})
+
+    def prefix_in(block):
+        held = prefix_half(block, c)
+        return remote(held, held, pz_send.at[block], pz_recv.at[block], {"path": block})
+
+    def prefix_share(block, core):
+        held = prefix_half(block, core)
+        return remote(held, held, ps_send.at[block], ps_recv.at[block], {"tile": sib})
+
+    def state_out(to):
+        return remote(
+            stage.at[to], right_st.at[part(z, c)], st_send.at[to], st_recv.at[z], {"path": to}
+        )
+
+    def state_in(block):
+        return remote(
+            stage.at[block], right_st.at[part(block, c)], st_send.at[block], st_recv.at[block],
+            {"path": block},
+        )
+
+    def state_share(block, core):
+        held = right_st.at[part(block, core)]
+        return remote(held, held, ss_send.at[block], ss_recv.at[block], {"tile": sib})
+
+    def each(d, do):
+        @pl.when(z >= d)
+        def _():
+            do(z - d)
+        @pl.when(z + d < n_path)
+        def _():
+            do(z + d)
+
+    own[1].wait()
+    for copy in prefix_copies[n_path - 1:]:
         copy.wait_recv()
-    for ref, rows, path_map in ((left_proj, left_rows, left_map), (right_proj, right_rows, right_map)):
-        chosen = picked_rows(rows, path_map[...])
-        ref[...] = (chosen * ref[...].astype(jnp.float32)).astype(jnp.bfloat16)
-
-    left.multiply(pl.ds(pl.multiple_of(mine * block_l, block_l), block_l))
-    right.multiply(pl.ds(pl.multiple_of(z * block_r, block_r), block_r))
-
-    slots = max(right.slots, left.slots)
-
-    def step(s, _):
-        right.relay(s)
+    def far_first(k, _):
+        each(n_path - 1 - k, lambda to: prefix_out(to).start())
+        return 0
+    if n_path > 1:
+        lax.fori_loop(0, n_path - 1, far_first, 0)
+
+    def project_right(block):
+        chosen = picked_rows(right_rows[block], right_map[...])
+        right_proj[...] = (chosen * right_factor[...].astype(jnp.float32)).astype(jnp.bfloat16)
+
+    def right_times(rows):
+        return lax.dot_general(
+            rows, right_proj[...], NT, preferred_element_type=jnp.float32
+        ).astype(jnp.bfloat16)
+
+    own[0].wait()
+    for copy in prefix_copies[:n_path - 1]:
+        copy.wait_recv()
+    chosen = picked_rows(left_rows[...], left_map[...])
+    left_proj[...] = (chosen * left_proj[...].astype(jnp.float32)).astype(jnp.bfloat16)
+    own[2].wait()
+    own[3].wait()
+
+    def right_step(d):
+        def pass_on(block):
+            prefix_in(block).wait_recv()
+            prefix_share(block, c).start()
+        each(d, pass_on)
+
+        def form(block):
+            prefix_share(block, sib).wait_recv()
+            project_right(block)
+            stage[block] = right_times(right_w[pl.ds(pl.multiple_of(c * part_r, part_r), part_r), :])
+            state_out(block).start()
+        each(d, form)
+
+    def left_step(s):
         left.relay(s)
-        right.compute_shared(s - 1)
         left.compute_shared(s - 1)
-        right.compute(s)
         left.compute(s)
+
+    project_right(z)
+    for core in range(n_tile):
+        right_st[part(z, core), :] = right_times(right_w[core * part_r:(core + 1) * part_r, :])
+        right_flush(z, core).start()
+    for i in range(count_l):
+        left.multiply(x, c, i)
+
+    steps = max(n_path - 1, left.slots)
+
+    def step(t, _):
+        @pl.when(t < n_path - 1)
+        def _():
+            right_step(t + 1)
+        left_step(t)
         return 0
 
     def shared_block():
         for i in range(count_l):
             own_share(i, sib).wait_recv()
-        left.multiply(pl.ds(pl.multiple_of((x * n_tile + sib) * block_l, block_l), block_l))
-
-    if slots > 0:
-        lax.fori_loop(0, 1, step, 0)
+            left.multiply(x, sib, i)
+
     shared_block()
-    if slots > 1:
-        lax.fori_loop(1, slots, step, 0)
-    right.compute_shared(jnp.int32(slots - 1))
-    left.compute_shared(jnp.int32(slots - 1))
-
-    for line in (right, left):
-        if line.slots > 0:
-            lax.fori_loop(0, line.slots, lambda s, _, line=line: (line.finish(s), 0)[1], 0)
+    both = min(n_path - 1, left.slots)
+    if both > 0:
+        lax.fori_loop(0, both, step, 0)
+    if n_path - 1 > both:
+        lax.fori_loop(both, n_path - 1, lambda t, _: (right_step(t + 1), 0)[1], 0)
+
+    def take(k, _):
+        def landed(block):
+            state_in(block).wait_recv()
+            state_share(block, c).start()
+            right_flush(block, c).start()
+        each(k + 1, landed)
+        return 0
+
+    if n_path > 1:
+        lax.fori_loop(0, n_path - 1, take, 0)
+    if left.slots > both:
+        lax.fori_loop(both, left.slots, lambda t, _: (left_step(t), 0)[1], 0)
+
+    def take_shared(k, _):
+        def landed(block):
+            state_share(block, sib).wait_recv()
+            right_flush(block, sib).start()
+        each(k + 1, landed)
+        return 0
+
+    if n_path > 1:
+        lax.fori_loop(0, n_path - 1, take_shared, 0)
+    left.compute_shared(jnp.int32(left.slots - 1))
+
+    def close(k, _):
+        def ended(block):
+            prefix_out(block).wait_send()
+            prefix_share(block, c).wait_send()
+            state_out(block).wait_send()
+            state_share(block, c).wait_send()
+        each(k + 1, ended)
+        return 0
+
+    if n_path > 1:
+        lax.fori_loop(0, n_path - 1, close, 0)
+    if left.slots > 0:
+        lax.fori_loop(0, left.slots, lambda s, _: (left.finish(s), 0)[1], 0)
     for i in range(count_l):
         own_share(i, c).wait_send()
     for copy in prefix_copies:
         copy.wait_send()
+
+    def flushed_left(k, _):
+        for core in range(n_tile):
+            for i in range(count_l):
+                left_flush(k, core, i).wait()
+        return 0
+
+    def flushed_right(k, _):
+        for core in range(n_tile):
+            right_flush(k, core).wait()
+        return 0
+
+    lax.fori_loop(0, n_half, flushed_left, 0)
+    lax.fori_loop(0, n_path, flushed_right, 0)
 
 
 def on_device(
@@ -293,9 +428,7 @@
     gate = left_layer.shape[1]
     hi_l, hi_r = left_layer.shape[0] * n_lr, right_layer.shape[0] * n_path
     part_r = right_layer.shape[0] // n_tile
-    count_r = part_r // max(16, part_r // 2)
     count_l = left_layer.shape[0] // max(16, left_layer.shape[0] // 4)
-    slots_r = max(1, (n_path - 1) * count_r)
     slots_l = max(1, (n_half - 1) * count_l)
     pre = n_path + n_lr - 2
     dma = pltpu.SemaphoreType.DMA
@@ -308,23 +441,28 @@
             jax.ShapeDtypeStruct((hi_r, paths), jnp.bfloat16),
         ),
         in_specs=[anywhere] * 4 + [vmem] * 4,
-        out_specs=(vmem, vmem),
+        out_specs=(anywhere, anywhere),
         scratch_shapes=[
             pltpu.VMEM((n_path,) + left_prefix.shape, jnp.bfloat16),
-            pltpu.VMEM((n_lr,) + right_prefix.shape, jnp.bfloat16),
+            pltpu.VMEM((n_path, n_lr) + right_prefix.shape, jnp.bfloat16),
+            pltpu.VMEM((paths, gate), jnp.bfloat16),
             pltpu.VMEM((paths, gate), jnp.bfloat16),
             pltpu.VMEM((paths, gate), jnp.bfloat16),
             pltpu.VMEM((hi_l, gate), jnp.bfloat16),
-            pltpu.VMEM((hi_r, gate), jnp.bfloat16),
+            pltpu.VMEM(right_layer.shape, jnp.bfloat16),
+            pltpu.VMEM((hi_l, paths), jnp.bfloat16),
+            pltpu.VMEM((hi_r, paths), jnp.bfloat16),
+            pltpu.VMEM((n_path, part_r, paths), jnp.bfloat16),
             dma((4,)), dma((pre,)), dma((pre,)),
-            dma((2, slots_r)), dma((2, slots_r)), dma((2, slots_r)), dma((2, slots_r)),
+        ] + [dma((n_path,))] * 8 + [
             dma((2, slots_l)), dma((2, slots_l)), dma((2, slots_l)), dma((2, slots_l)),
             dma((count_l,)), dma((count_l,)),
+            dma((n_lr * count_l,)), dma((n_path * n_tile,)),
         ],
         compiler_params=pltpu.CompilerParams(collective_id=0, has_side_effects=True),
     )(
         left_prefix, right_prefix, left_layer, right_layer,
-        left_map[None, :], right_map[None, :], branch_bits, cut_side[None, :],
+        left_map[None, :], right_map[None, :], branch_bits.T, cut_side[None, :],
     )
     amplitude = lax.dot_general(
         left_states, right_states, NT, preferred_element_type=jnp.float32

time: 33.4 us -> 29.5 us (0.88)
  Pallas kernels: 28.4 us -> 26.1 us
  local copies, waits for them, and re-layouts: 1.48 us -> 0 us
    pallas_call x1, Pallas kernels: 28.4 us -> 26.1 us  [on_device(): pl.pallas_call(functools.partial(kernel, sizes), out_shape=(jax.ShapeDtyp...]
    unnamed x1 -> x0, local copies, waits for them, and re-layouts: 1.48 us -> none
where the time goes in v2:
time: 29.5 us; the launch traced here: 29.4 us
  Pallas kernels  26.1 us (88%)
  matrix products  3.26 us (11%)
    pallas_call x1, Pallas kernels, on_device(): pl.pallas_call(functools.partial(kernel, sizes), out_shape=(jax.ShapeDtyp...  26.1 us
    dot_general x1, matrix products, on_device(): lax.dot_general(left_states, right_states, NT, preferred_element_type=jnp...  3.26 us

profile of v2, /device:TPU:1, one launch (start us, length us, event | category | flops | bytes accessed | tf_op | source)
XLA Modules:
  0.0 29.4 jit_solution(17616765876064909808)
XLA Ops:
  0.0 26.1 %shard_map.82 = (bf16[1024,256]{1,0:T(8,128)(2,1)}, bf16[1024,256]{1,0:T(8,128)(2,1)}) custom-call(bf16[8,1024]{1,0:T(8,128)(2,1)} %left_prefix.1, bf16[8,1024]{1,0:T(8,128)(2,1)} %right_prefix.1, bf16[256,1024]{1,0:T(8,128)(2,1)} %left_layer.1, bf16[256,1024]{1,0:T(8,128)(2,1)} %right_layer.1, s32[1,256]{1,0:T(1,128)} %bitcast.7, s32[1,256]{1,0:T(1,128)} %bitcast.8, ...), custom_call_target="tpu_custom_call" | custom-call | tf_op jit(solution)/shard_map/pallas_call | solution.py:437
  26.1 3.3 %convolution_convert_fusion = bf16[1024,1024]{1,0:T(8,128)(2,1)} fusion(bf16[1024,256]{1,0:T(8,128)(2,1)} %get-tuple-element.7, bf16[1024,256]{1,0:T(8,128)(2,1)} %get-tuple-element.8), kind=kOutput, calls=%fused_computation | convolution fusion | flops 537919488 | bytes 3145728 | tf_op jit(solution)/shard_map/dot_general | solution.py:467

commit v3 on v2

--- a/solution.py
+++ b/solution.py
@@ -37,14 +37,14 @@
     return made
 
 
-def picked_rows(prefix, path_map):
-    shards, rows, gate_count = prefix.shape
-    prefix = prefix.astype(jnp.float32).reshape(shards * rows, gate_count)
-    which = lax.broadcasted_iota(jnp.int32, (shards * rows, path_map.shape[1]), 0)
-    hot = jnp.where(which == path_map, 1.0, 0.0).T
-    return jnp.dot(
-        hot.astype(jnp.bfloat16), prefix.astype(jnp.bfloat16), preferred_element_type=jnp.float32
-    )
+def one_hot(which, path_map):
+    return jnp.where(which == path_map, 1.0, 0.0).T.astype(jnp.bfloat16)
+
+
+def picked_rows(hot, prefix):
+    gate_count = prefix.shape[-1]
+    rows = prefix.astype(jnp.float32).reshape(-1, gate_count).astype(jnp.bfloat16)
+    return jnp.dot(hot, rows, preferred_element_type=jnp.float32)
 
 
 def kernel(
@@ -52,7 +52,7 @@
     left_prefix, right_prefix, left_layer, right_layer, left_map, right_map, branch_bits, cut_side,
     left_out, right_out,
     left_rows, right_rows, left_proj, right_factor, right_proj, left_w, right_w,
-    left_st, right_st, stage,
+    left_st, right_st, stage, hot_l, hot_r,
     own_sem, pre_send, pre_recv,
     pz_send, pz_recv, ps_send, ps_recv,
     st_send, st_recv, ss_send, ss_recv,
@@ -65,29 +65,27 @@
     mine = x * n_tile + c
 
     barrier = pltpu.get_barrier_semaphore()
-    for k in range(1, n_path):
-        pl.semaphore_signal(
-            barrier, inc=1, device_id={"path": lax.rem(z + k, n_path)}, device_id_type=MESH
-        )
-    for k in range(1, n_lr):
-        there = lax.rem(mine + k, n_lr)
-        pl.semaphore_signal(
-            barrier,
-            inc=1,
-            device_id={"half": there // n_tile, "tile": lax.rem(there, n_tile)},
-            device_id_type=MESH,
-        )
+
+    def chips(do):
+        for dz in range(n_path - 1, -1, -1):
+            for dx in range(n_half):
+                if dz or dx:
+                    do(lax.rem(x + dx, n_half), lax.rem(z + dz, n_path))
+
+    chips(lambda tx, tz: pl.semaphore_signal(
+        barrier, inc=1, device_id={"half": tx, "path": tz}, device_id_type=MESH
+    ))
+    pl.semaphore_signal(barrier, inc=1, device_id={"tile": sib}, device_id_type=MESH)
 
     block_l, gate = left_layer.shape
     block_r = right_layer.shape[0]
     part_r = block_r // n_tile
     chunk_l = max(16, block_l // 4)
     count_l = block_l // chunk_l
-    half_lr = n_lr // n_tile
 
     own = [
         pltpu.make_async_copy(left_prefix, left_rows.at[z], own_sem.at[0]),
-        pltpu.make_async_copy(right_prefix, right_rows.at[z, mine], own_sem.at[1]),
+        pltpu.make_async_copy(right_prefix, right_rows.at[z, c, x], own_sem.at[1]),
         pltpu.make_async_copy(
             left_layer, left_w.at[pl.ds(pl.multiple_of(mine * block_l, block_l), block_l)], own_sem.at[2]
         ),
@@ -96,31 +94,34 @@
     for copy in own:
         copy.start()
 
-    side = cut_side[...].astype(jnp.float32)
-    branch = branch_bits[...].astype(jnp.float32)
-    for ref, factor in zip((left_proj, right_factor), factors(branch, side, gate)):
-        ref[...] = factor.astype(jnp.bfloat16)
-
-    pl.semaphore_wait(barrier, n_path - 1 + n_lr - 1)
+    pl.semaphore_wait(barrier, n_path * n_half)
 
     def remote(src, dst, send, recv, device):
         return pltpu.make_async_remote_copy(
             src_ref=src, dst_ref=dst, send_sem=send, recv_sem=recv, device_id=device, device_id_type=MESH
         )
 
-    prefix_copies = []
-    for k in range(1, n_path):
-        prefix_copies.append(remote(
+    def prefix_out(tx, tz):
+        return remote(
+            right_prefix, right_rows.at[z, c, x], pz_send.at[tz * n_half + tx],
+            pz_recv.at[z * n_half + x], {"half": tx, "path": tz},
+        )
+
+    def prefix_in(fx, fz):
+        held = right_rows.at[fz, c, fx]
+        return remote(
+            held, held, pz_send.at[fz * n_half + fx], pz_recv.at[fz * n_half + fx],
+            {"half": fx, "path": fz},
+        )
+
+    chips(lambda tx, tz: prefix_out(tx, tz).start())
+    prefix_copies = [
+        remote(
             left_prefix, left_rows.at[z], pre_send.at[k - 1], pre_recv.at[k - 1],
             {"path": lax.rem(z + k, n_path)},
-        ))
-    for k in range(1, n_lr):
-        there = lax.rem(mine + k, n_lr)
-        slot = n_path - 1 + k - 1
-        prefix_copies.append(remote(
-            right_prefix, right_rows.at[z, mine], pre_send.at[slot], pre_recv.at[slot],
-            {"half": there // n_tile, "tile": lax.rem(there, n_tile)},
-        ))
+        )
+        for k in range(1, n_path)
+    ]
     for copy in prefix_copies:
         copy.start()
 
@@ -251,19 +252,24 @@
     for i in range(count_l):
         own_share(i, c).start()
 
-    def prefix_half(block, core):
-        return right_rows.at[block, pl.ds(core * half_lr, half_lr)]
-
-    def prefix_out(to):
-        held = prefix_half(z, c)
-        return remote(held, held, pz_send.at[to], pz_recv.at[z], {"path": to})
-
-    def prefix_in(block):
-        held = prefix_half(block, c)
-        return remote(held, held, pz_send.at[block], pz_recv.at[block], {"path": block})
+    side = cut_side[...].astype(jnp.float32)
+    branch = branch_bits[...].astype(jnp.float32)
+    for ref, factor in zip((left_proj, right_factor), factors(branch, side, gate)):
+        ref[...] = factor.astype(jnp.bfloat16)
+
+    shard = left_prefix.shape[0]
+    paths = left_map.shape[1]
+    hot_l[...] = one_hot(
+        lax.broadcasted_iota(jnp.int32, (n_path * shard, paths), 0), left_map[...]
+    )
+    shard = right_prefix.shape[0]
+    dims = (n_tile, n_half, shard, paths)
+    core_at, half_at, row_at = (lax.broadcasted_iota(jnp.int32, dims, k) for k in range(3))
+    which = (half_at * n_tile + core_at) * shard + row_at
+    hot_r[...] = one_hot(which.reshape(n_lr * shard, paths), right_map[...])
 
     def prefix_share(block, core):
-        held = prefix_half(block, core)
+        held = right_rows.at[block, core]
         return remote(held, held, ps_send.at[block], ps_recv.at[block], {"tile": sib})
 
     def state_out(to):
@@ -290,16 +296,12 @@
             do(z + d)
 
     own[1].wait()
-    for copy in prefix_copies[n_path - 1:]:
-        copy.wait_recv()
-    def far_first(k, _):
-        each(n_path - 1 - k, lambda to: prefix_out(to).start())
-        return 0
-    if n_path > 1:
-        lax.fori_loop(0, n_path - 1, far_first, 0)
+    for dx in range(1, n_half):
+        prefix_in(lax.rem(x + dx, n_half), z).wait_recv()
+    prefix_share(z, c).start()
 
     def project_right(block):
-        chosen = picked_rows(right_rows[block], right_map[...])
+        chosen = picked_rows(hot_r[...], right_rows[block])
         right_proj[...] = (chosen * right_factor[...].astype(jnp.float32)).astype(jnp.bfloat16)
 
     def right_times(rows):
@@ -308,16 +310,17 @@
         ).astype(jnp.bfloat16)
 
     own[0].wait()
-    for copy in prefix_copies[:n_path - 1]:
+    for copy in prefix_copies:
         copy.wait_recv()
-    chosen = picked_rows(left_rows[...], left_map[...])
+    chosen = picked_rows(hot_l[...], left_rows[...])
     left_proj[...] = (chosen * left_proj[...].astype(jnp.float32)).astype(jnp.bfloat16)
     own[2].wait()
     own[3].wait()
 
     def right_step(d):
         def pass_on(block):
-            prefix_in(block).wait_recv()
+            for fx in range(n_half):
+                prefix_in(fx, block).wait_recv()
             prefix_share(block, c).start()
         each(d, pass_on)
 
@@ -333,6 +336,7 @@
         left.compute_shared(s - 1)
         left.compute(s)
 
+    prefix_share(z, sib).wait_recv()
     project_right(z)
     for core in range(n_tile):
         right_st[part(z, core), :] = right_times(right_w[core * part_r:(core + 1) * part_r, :])
@@ -387,7 +391,6 @@
 
     def close(k, _):
         def ended(block):
-            prefix_out(block).wait_send()
             prefix_share(block, c).wait_send()
             state_out(block).wait_send()
             state_share(block, c).wait_send()
@@ -400,6 +403,8 @@
         lax.fori_loop(0, left.slots, lambda s, _: (left.finish(s), 0)[1], 0)
     for i in range(count_l):
         own_share(i, c).wait_send()
+    chips(lambda tx, tz: prefix_out(tx, tz).wait_send())
+    prefix_share(z, c).wait_send()
     for copy in prefix_copies:
         copy.wait_send()
 
@@ -430,7 +435,8 @@
     part_r = right_layer.shape[0] // n_tile
     count_l = left_layer.shape[0] // max(16, left_layer.shape[0] // 4)
     slots_l = max(1, (n_half - 1) * count_l)
-    pre = n_path + n_lr - 2
+    pre = max(1, n_path - 1)
+    chips = n_path * n_half
     dma = pltpu.SemaphoreType.DMA
     vmem = pl.BlockSpec(memory_space=pltpu.VMEM)
     anywhere = pl.BlockSpec(memory_space=pl.ANY)
@@ -444,7 +450,7 @@
         out_specs=(anywhere, anywhere),
         scratch_shapes=[
             pltpu.VMEM((n_path,) + left_prefix.shape, jnp.bfloat16),
-            pltpu.VMEM((n_path, n_lr) + right_prefix.shape, jnp.bfloat16),
+            pltpu.VMEM((n_path, n_tile, n_half) + right_prefix.shape, jnp.bfloat16),
             pltpu.VMEM((paths, gate), jnp.bfloat16),
             pltpu.VMEM((paths, gate), jnp.bfloat16),
             pltpu.VMEM((paths, gate), jnp.bfloat16),
@@ -453,8 +459,11 @@
             pltpu.VMEM((hi_l, paths), jnp.bfloat16),
             pltpu.VMEM((hi_r, paths), jnp.bfloat16),
             pltpu.VMEM((n_path, part_r, paths), jnp.bfloat16),
+            pltpu.VMEM((paths, left_prefix.shape[0] * n_path), jnp.bfloat16),
+            pltpu.VMEM((paths, right_prefix.shape[0] * n_lr), jnp.bfloat16),
             dma((4,)), dma((pre,)), dma((pre,)),
-        ] + [dma((n_path,))] * 8 + [
+            dma((chips,)), dma((chips,)),
+        ] + [dma((n_path,))] * 6 + [
             dma((2, slots_l)), dma((2, slots_l)), dma((2, slots_l)), dma((2, slots_l)),
             dma((count_l,)), dma((count_l,)),
             dma((n_lr * count_l,)), dma((n_path * n_tile,)),

time: 29.5 us -> 31.4 us (1.064)
  Pallas kernels: 26.1 us -> 27.7 us
    pallas_call x1, Pallas kernels: 26.1 us -> 27.7 us  [on_device(): pl.pallas_call(functools.partial(kernel, sizes), out_shape=(jax.ShapeDtyp...]
where the time goes in v3:
time: 31.4 us; the launch traced here: 31 us
  Pallas kernels  27.7 us (88%)
  matrix products  3.26 us (10%)
    pallas_call x1, Pallas kernels, on_device(): pl.pallas_call(functools.partial(kernel, sizes), out_shape=(jax.ShapeDtyp...  27.7 us
    dot_general x1, matrix products, on_device(): lax.dot_general(left_states, right_states, NT, preferred_element_type=jnp...  3.26 us

profile of v3, /device:TPU:1, one launch (start us, length us, event | category | flops | bytes accessed | tf_op | source)
XLA Modules:
  0.0 31.0 jit_solution(18133481382614073075)
XLA Ops:
  0.0 27.7 %shard_map.82 = (bf16[1024,256]{1,0:T(8,128)(2,1)}, bf16[1024,256]{1,0:T(8,128)(2,1)}) custom-call(bf16[8,1024]{1,0:T(8,128)(2,1)} %left_prefix.1, bf16[8,1024]{1,0:T(8,128)(2,1)} %right_prefix.1, bf16[256,1024]{1,0:T(8,128)(2,1)} %left_layer.1, bf16[256,1024]{1,0:T(8,128)(2,1)} %right_layer.1, s32[1,256]{1,0:T(1,128)} %bitcast.7, s32[1,256]{1,0:T(1,128)} %bitcast.8, ...), custom_call_target="tpu_custom_call" | custom-call | tf_op jit(solution)/shard_map/pallas_call | solution.py:443
  27.7 3.3 %convolution_convert_fusion = bf16[1024,1024]{1,0:T(8,128)(2,1)} fusion(bf16[1024,256]{1,0:T(8,128)(2,1)} %get-tuple-element.7, bf16[1024,256]{1,0:T(8,128)(2,1)} %get-tuple-element.8), kind=kOutput, calls=%fused_computation | convolution fusion | flops 537919488 | bytes 3145728 | tf_op jit(solution)/shard_map/dot_general | solution.py:476

commit v4 on v2

--- a/solution.py
+++ b/solution.py
@@ -37,14 +37,15 @@
     return made
 
 
-def picked_rows(prefix, path_map):
-    shards, rows, gate_count = prefix.shape
-    prefix = prefix.astype(jnp.float32).reshape(shards * rows, gate_count)
-    which = lax.broadcasted_iota(jnp.int32, (shards * rows, path_map.shape[1]), 0)
-    hot = jnp.where(which == path_map, 1.0, 0.0).T
-    return jnp.dot(
-        hot.astype(jnp.bfloat16), prefix.astype(jnp.bfloat16), preferred_element_type=jnp.float32
-    )
+def one_hot(rows, path_map):
+    which = lax.broadcasted_iota(jnp.int32, (rows, path_map.shape[1]), 0)
+    return jnp.where(which == path_map, 1.0, 0.0).T.astype(jnp.bfloat16)
+
+
+def picked_rows(hot, prefix):
+    gate_count = prefix.shape[-1]
+    rows = prefix.astype(jnp.float32).reshape(-1, gate_count).astype(jnp.bfloat16)
+    return jnp.dot(hot, rows, preferred_element_type=jnp.float32)
 
 
 def kernel(
@@ -52,7 +53,7 @@
     left_prefix, right_prefix, left_layer, right_layer, left_map, right_map, branch_bits, cut_side,
     left_out, right_out,
     left_rows, right_rows, left_proj, right_factor, right_proj, left_w, right_w,
-    left_st, right_st, stage,
+    left_st, right_st, stage, hot_l, hot_r, told,
     own_sem, pre_send, pre_recv,
     pz_send, pz_recv, ps_send, ps_recv,
     st_send, st_recv, ss_send, ss_recv,
@@ -65,10 +66,17 @@
     mine = x * n_tile + c
 
     barrier = pltpu.get_barrier_semaphore()
-    for k in range(1, n_path):
-        pl.semaphore_signal(
-            barrier, inc=1, device_id={"path": lax.rem(z + k, n_path)}, device_id_type=MESH
-        )
+    def neighbours(do):
+        @pl.when(z >= 1)
+        def _():
+            do(z - 1, 1)
+        @pl.when(z + 1 < n_path)
+        def _():
+            do(z + 1, 0)
+
+    neighbours(lambda there, _: pl.semaphore_signal(
+        barrier, inc=1, device_id={"path": there}, device_id_type=MESH
+    ))
     for k in range(1, n_lr):
         there = lax.rem(mine + k, n_lr)
         pl.semaphore_signal(
@@ -101,7 +109,24 @@
     for ref, factor in zip((left_proj, right_factor), factors(branch, side, gate)):
         ref[...] = factor.astype(jnp.bfloat16)
 
-    pl.semaphore_wait(barrier, n_path - 1 + n_lr - 1)
+    beside = (z >= 1).astype(jnp.int32) + (z + 1 < n_path).astype(jnp.int32)
+    pl.semaphore_wait(barrier, beside + n_lr - 1)
+
+    def tell():
+        neighbours(lambda there, way: pl.semaphore_signal(
+            told.at[way], inc=1, device_id={"path": there}, device_id_type=MESH
+        ))
+
+    def hear():
+        @pl.when(z >= 1)
+        def _():
+            pl.semaphore_wait(told.at[0], 1)
+        @pl.when(z + 1 < n_path)
+        def _():
+            pl.semaphore_wait(told.at[1], 1)
+
+    if n_path > 2:
+        tell()
 
     def remote(src, dst, send, recv, device):
         return pltpu.make_async_remote_copy(
@@ -121,7 +146,7 @@
             right_prefix, right_rows.at[z, mine], pre_send.at[slot], pre_recv.at[slot],
             {"half": there // n_tile, "tile": lax.rem(there, n_tile)},
         ))
-    for copy in prefix_copies:
+    for copy in prefix_copies[n_path - 1:]:
         copy.start()
 
     def rows_l(block, core, i):
@@ -251,6 +276,16 @@
     for i in range(count_l):
         own_share(i, c).start()
 
+    hot_l[...] = one_hot(hot_l.shape[1], left_map[...])
+    hot_r[...] = one_hot(hot_r.shape[1], right_map[...])
+    if n_path > 2:
+        hear()
+        for _ in range(n_path - 3):
+            tell()
+            hear()
+    for copy in prefix_copies[:n_path - 1]:
+        copy.start()
+
     def prefix_half(block, core):
         return right_rows.at[block, pl.ds(core * half_lr, half_lr)]
 
@@ -299,7 +334,7 @@
         lax.fori_loop(0, n_path - 1, far_first, 0)
 
     def project_right(block):
-        chosen = picked_rows(right_rows[block], right_map[...])
+        chosen = picked_rows(hot_r[...], right_rows[block])
         right_proj[...] = (chosen * right_factor[...].astype(jnp.float32)).astype(jnp.bfloat16)
 
     def right_times(rows):
@@ -310,7 +345,7 @@
     own[0].wait()
     for copy in prefix_copies[:n_path - 1]:
         copy.wait_recv()
-    chosen = picked_rows(left_rows[...], left_map[...])
+    chosen = picked_rows(hot_l[...], left_rows[...])
     left_proj[...] = (chosen * left_proj[...].astype(jnp.float32)).astype(jnp.bfloat16)
     own[2].wait()
     own[3].wait()
@@ -453,6 +488,9 @@
             pltpu.VMEM((hi_l, paths), jnp.bfloat16),
             pltpu.VMEM((hi_r, paths), jnp.bfloat16),
             pltpu.VMEM((n_path, part_r, paths), jnp.bfloat16),
+            pltpu.VMEM((paths, left_prefix.shape[0] * n_path), jnp.bfloat16),
+            pltpu.VMEM((paths, right_prefix.shape[0] * n_lr), jnp.bfloat16),
+            pltpu.SemaphoreType.REGULAR((2,)),
             dma((4,)), dma((pre,)), dma((pre,)),
         ] + [dma((n_path,))] * 8 + [
             dma((2, slots_l)), dma((2, slots_l)), dma((2, slots_l)), dma((2, slots_l)),

time: 29.5 us -> 31.5 us (1.068)
  Pallas kernels: 26.1 us -> 27.8 us
    pallas_call x1, Pallas kernels: 26.1 us -> 27.8 us  [on_device(): pl.pallas_call(functools.partial(kernel, sizes), out_shape=(jax.ShapeDtyp...]
where the time goes in v4:
time: 31.5 us; the launch traced here: 31 us
  Pallas kernels  27.8 us (88%)
  matrix products  3.26 us (10%)
    pallas_call x1, Pallas kernels, on_device(): pl.pallas_call(functools.partial(kernel, sizes), out_shape=(jax.ShapeDtyp...  27.8 us
    dot_general x1, matrix products, on_device(): lax.dot_general(left_states, right_states, NT, preferred_element_type=jnp...  3.26 us

profile of v4, /device:TPU:1, one launch (start us, length us, event | category | flops | bytes accessed | tf_op | source)
XLA Modules:
  0.0 31.0 jit_solution(7316466079953070796)
XLA Ops:
  0.0 27.8 %shard_map.82 = (bf16[1024,256]{1,0:T(8,128)(2,1)}, bf16[1024,256]{1,0:T(8,128)(2,1)}) custom-call(bf16[8,1024]{1,0:T(8,128)(2,1)} %left_prefix.1, bf16[8,1024]{1,0:T(8,128)(2,1)} %right_prefix.1, bf16[256,1024]{1,0:T(8,128)(2,1)} %left_layer.1, bf16[256,1024]{1,0:T(8,128)(2,1)} %right_layer.1, s32[1,256]{1,0:T(1,128)} %bitcast.7, s32[1,256]{1,0:T(1,128)} %bitcast.8, ...), custom_call_target="tpu_custom_call" | custom-call | tf_op jit(solution)/shard_map/pallas_call | solution.py:472
  27.8 3.3 %convolution_convert_fusion = bf16[1024,1024]{1,0:T(8,128)(2,1)} fusion(bf16[1024,256]{1,0:T(8,128)(2,1)} %get-tuple-element.7, bf16[1024,256]{1,0:T(8,128)(2,1)} %get-tuple-element.8), kind=kOutput, calls=%fused_computation | convolution fusion | flops 537919488 | bytes 3145728 | tf_op jit(solution)/shard_map/dot_general | solution.py:505

commit v5 on v4

--- a/solution.py
+++ b/solution.py
@@ -283,9 +283,6 @@
         for _ in range(n_path - 3):
             tell()
             hear()
-    for copy in prefix_copies[:n_path - 1]:
-        copy.start()
-
     def prefix_half(block, core):
         return right_rows.at[block, pl.ds(core * half_lr, half_lr)]
 
@@ -333,6 +330,9 @@
     if n_path > 1:
         lax.fori_loop(0, n_path - 1, far_first, 0)
 
+    for copy in prefix_copies[:n_path - 1]:
+        copy.start()
+
     def project_right(block):
         chosen = picked_rows(hot_r[...], right_rows[block])
         right_proj[...] = (chosen * right_factor[...].astype(jnp.float32)).astype(jnp.bfloat16)
@@ -341,6 +341,32 @@
         return lax.dot_general(
             rows, right_proj[...], NT, preferred_element_type=jnp.float32
         ).astype(jnp.bfloat16)
+
+    def right_step(d):
+        def pass_on(block):
+            prefix_in(block).wait_recv()
+            prefix_share(block, c).start()
+        each(d, pass_on)
+
+        def form(block):
+            prefix_share(block, sib).wait_recv()
+            project_right(block)
+            stage[block] = right_times(right_w[pl.ds(pl.multiple_of(c * part_r, part_r), part_r), :])
+            state_out(block).start()
+        each(d, form)
+
+    def left_step(s):
+        left.relay(s)
+        left.compute_shared(s - 1)
+        left.compute(s)
+
+    own[3].wait()
+    project_right(z)
+    for core in range(n_tile):
+        right_st[part(z, core), :] = right_times(right_w[core * part_r:(core + 1) * part_r, :])
+        right_flush(z, core).start()
+    if n_path > 1:
+        lax.fori_loop(0, n_path - 1, lambda t, _: (right_step(t + 1), 0)[1], 0)
 
     own[0].wait()
     for copy in prefix_copies[:n_path - 1]:
@@ -348,53 +374,13 @@
     chosen = picked_rows(hot_l[...], left_rows[...])
     left_proj[...] = (chosen * left_proj[...].astype(jnp.float32)).astype(jnp.bfloat16)
     own[2].wait()
-    own[3].wait()
-
-    def right_step(d):
-        def pass_on(block):
-            prefix_in(block).wait_recv()
-            prefix_share(block, c).start()
-        each(d, pass_on)
-
-        def form(block):
-            prefix_share(block, sib).wait_recv()
-            project_right(block)
-            stage[block] = right_times(right_w[pl.ds(pl.multiple_of(c * part_r, part_r), part_r), :])
-            state_out(block).start()
-        each(d, form)
-
-    def left_step(s):
-        left.relay(s)
-        left.compute_shared(s - 1)
-        left.compute(s)
-
-    project_right(z)
-    for core in range(n_tile):
-        right_st[part(z, core), :] = right_times(right_w[core * part_r:(core + 1) * part_r, :])
-        right_flush(z, core).start()
     for i in range(count_l):
         left.multiply(x, c, i)
-
-    steps = max(n_path - 1, left.slots)
-
-    def step(t, _):
-        @pl.when(t < n_path - 1)
-        def _():
-            right_step(t + 1)
-        left_step(t)
-        return 0
-
-    def shared_block():
-        for i in range(count_l):
-            own_share(i, sib).wait_recv()
-            left.multiply(x, sib, i)
-
-    shared_block()
-    both = min(n_path - 1, left.slots)
-    if both > 0:
-        lax.fori_loop(0, both, step, 0)
-    if n_path - 1 > both:
-        lax.fori_loop(both, n_path - 1, lambda t, _: (right_step(t + 1), 0)[1], 0)
+    for i in range(count_l):
+        own_share(i, sib).wait_recv()
+        left.multiply(x, sib, i)
+    if left.slots > 0:
+        lax.fori_loop(0, left.slots, lambda t, _: (left_step(t), 0)[1], 0)
 
     def take(k, _):
         def landed(block):
@@ -406,9 +392,6 @@
 
     if n_path > 1:
         lax.fori_loop(0, n_path - 1, take, 0)
-    if left.slots > both:
-        lax.fori_loop(both, left.slots, lambda t, _: (left_step(t), 0)[1], 0)
-
     def take_shared(k, _):
         def landed(block):
             state_share(block, sib).wait_recv()

time: 31.5 us -> 29.4 us (0.933)
  Pallas kernels: 27.8 us -> 25.9 us
    pallas_call x1, Pallas kernels: 27.8 us -> 25.9 us  [on_device(): pl.pallas_call(functools.partial(kernel, sizes), out_shape=(jax.ShapeDtyp...]
where the time goes in v5:
time: 29.4 us; the launch traced here: 29.2 us
  Pallas kernels  25.9 us (88%)
  matrix products  3.26 us (11%)
    pallas_call x1, Pallas kernels, on_device(): pl.pallas_call(functools.partial(kernel, sizes), out_shape=(jax.ShapeDtyp...  25.9 us
    dot_general x1, matrix products, on_device(): lax.dot_general(left_states, right_states, NT, preferred_element_type=jnp...  3.26 us

profile of v5, /device:TPU:1, one launch (start us, length us, event | category | flops | bytes accessed | tf_op | source)
XLA Modules:
  0.0 29.2 jit_solution(17997841999456561907)
XLA Ops:
  0.0 25.9 %shard_map.82 = (bf16[1024,256]{1,0:T(8,128)(2,1)}, bf16[1024,256]{1,0:T(8,128)(2,1)}) custom-call(bf16[8,1024]{1,0:T(8,128)(2,1)} %left_prefix.1, bf16[8,1024]{1,0:T(8,128)(2,1)} %right_prefix.1, bf16[256,1024]{1,0:T(8,128)(2,1)} %left_layer.1, bf16[256,1024]{1,0:T(8,128)(2,1)} %right_layer.1, s32[1,256]{1,0:T(1,128)} %bitcast.7, s32[1,256]{1,0:T(1,128)} %bitcast.8, ...), custom_call_target="tpu_custom_call" | custom-call | tf_op jit(solution)/shard_map/pallas_call | solution.py:455
  25.9 3.3 %convolution_convert_fusion = bf16[1024,1024]{1,0:T(8,128)(2,1)} fusion(bf16[1024,256]{1,0:T(8,128)(2,1)} %get-tuple-element.7, bf16[1024,256]{1,0:T(8,128)(2,1)} %get-tuple-element.8), kind=kOutput, calls=%fused_computation | convolution fusion | flops 537919488 | bytes 3145728 | tf_op jit(solution)/shard_map/dot_general | solution.py:488

commit v6 on v5

--- a/solution.py
+++ b/solution.py
@@ -348,6 +348,7 @@
             prefix_share(block, c).start()
         each(d, pass_on)
 
+    def right_form(d):
         def form(block):
             prefix_share(block, sib).wait_recv()
             project_right(block)
@@ -367,6 +368,7 @@
         right_flush(z, core).start()
     if n_path > 1:
         lax.fori_loop(0, n_path - 1, lambda t, _: (right_step(t + 1), 0)[1], 0)
+        lax.fori_loop(0, n_path - 1, lambda t, _: (right_form(t + 1), 0)[1], 0)
 
     own[0].wait()
     for copy in prefix_copies[:n_path - 1]:

time: 29.4 us -> 29.4 us (level)
  no operation moved by 1% of the time
where the time goes in v6:
time: 29.4 us; the launch traced here: 29.2 us
  Pallas kernels  25.9 us (88%)
  matrix products  3.26 us (11%)
    pallas_call x1, Pallas kernels, on_device(): pl.pallas_call(functools.partial(kernel, sizes), out_shape=(jax.ShapeDtyp...  25.9 us
    dot_general x1, matrix products, on_device(): lax.dot_general(left_states, right_states, NT, preferred_element_type=jnp...  3.26 us

profile of v6, /device:TPU:1, one launch (start us, length us, event | category | flops | bytes accessed | tf_op | source)
XLA Modules:
  0.0 29.2 jit_solution(3170940135365832181)
XLA Ops:
  0.0 25.9 %shard_map.82 = (bf16[1024,256]{1,0:T(8,128)(2,1)}, bf16[1024,256]{1,0:T(8,128)(2,1)}) custom-call(bf16[8,1024]{1,0:T(8,128)(2,1)} %left_prefix.1, bf16[8,1024]{1,0:T(8,128)(2,1)} %right_prefix.1, bf16[256,1024]{1,0:T(8,128)(2,1)} %left_layer.1, bf16[256,1024]{1,0:T(8,128)(2,1)} %right_layer.1, s32[1,256]{1,0:T(1,128)} %bitcast.7, s32[1,256]{1,0:T(1,128)} %bitcast.8, ...), custom_call_target="tpu_custom_call" | custom-call | tf_op jit(solution)/shard_map/pallas_call | solution.py:457
  25.9 3.3 %convolution_convert_fusion = bf16[1024,1024]{1,0:T(8,128)(2,1)} fusion(bf16[1024,256]{1,0:T(8,128)(2,1)} %get-tuple-element.7, bf16[1024,256]{1,0:T(8,128)(2,1)} %get-tuple-element.8), kind=kOutput, calls=%fused_computation | convolution fusion | flops 537919488 | bytes 3145728 | tf_op jit(solution)/shard_map/dot_general | solution.py:490
